TPU v7x, 512 devices: a whole 4x4x16 slice. The times are simulated.
512 devices in a mesh: segment: 8 (over x, core), frames: 64 (over y, z).
Axes of the slice: x: 4, y: 4, z: 16, core: 2. Of those that a mesh axis runs over, the one named last changes fastest.
Arguments:
- hidden: bfloat16 [8, 16384, 1536], P('segment', 'frames'), may hold values from -3 to 3
- features: bfloat16 [4096, 768], P('frames'), may hold values from -160 to 160, as said below
- kv_weight: bfloat16 [8, 768, 3072], P('segment', None, 'frames'), may hold values from -0.21875 to 0.21875
- mod_table: float32 [8, 32, 3, 1536], P('segment'), may hold values from -4 to 4
- timestep: int32 [8, 256], P('segment', 'frames'), may hold values from 0 to 31
- block_list: int32 [8, 256, 4], P('segment', 'frames'), may hold values from 0 to 63
- block_count: int32 [8, 256], P('segment', 'frames'), may hold values from 1 to 4, as said below
Outputs:
- handed: bfloat16 [8, 16384, 1536], P('segment', 'frames')
Inputs may be any that keep to these rules, and one draw needn't show every extreme that they name: `features`: drawn as normal values, rows may carry common scales; within the bounds given. `block_list`: entry j of a block's list counts when j < the block's count; the others are ignored. `block_count`: the 4 frame blocks of one device have at most 10 live list entries together, and in every section some device has exactly 10.
All inputs are finite; a program needn't handle non-finite values.
Results may differ from a plain program's by a relative error of at most 0.0044.
The roundings to bfloat16 on the way count: a program that leaves them out, or rounds other values in their place, can miss the bound.
Values may be sent and summed in bfloat16 or wider, within the bound.
No kernel may reach another device: no remote copies, remote signals or barrier semaphores. Data moves between devices by JAX's collectives and lax.ppermute only.
A program may use at most 64 MiB of HBM per device.

v0:
```python
import jax
import jax.numpy as jnp
from jax import lax
from jax.sharding import PartitionSpec as P

HEADS = 12
HD = 128
BLK = 64


def from_behind(block, axis, distance):
    devices = range(lax.axis_size(axis))
    route = [((i - distance) % len(devices), i) for i in devices]
    return lax.ppermute(block, axis, route)


def local(hidden, features, kv_weight, mod_table, timestep, block_list, block_count):
    feature_table = lax.all_gather(features, "frames", axis=0, tiled=True)
    stream = hidden[0].astype(jnp.float32)
    tok_rows = stream.shape[0]
    feature_width = stream.shape[1]
    blocks_here = tok_rows // BLK
    normed = stream * lax.rsqrt(jnp.mean(stream * stream, axis=-1, keepdims=True) + 1e-06)
    levels = mod_table.shape[1]
    onehot = (timestep[0][:, None] == jnp.arange(levels, dtype=jnp.int32)[None, :]).astype(
        jnp.float32
    )
    modulate = jnp.sum(onehot[:, :, None, None] * mod_table[0][None], axis=1)
    normed_blocks = normed.reshape(blocks_here, BLK, feature_width)
    queries = (
        normed_blocks * (1.0 + modulate[:, 1][:, None, :]) + modulate[:, 0][:, None, :]
    ).astype(jnp.bfloat16)
    queries = queries.reshape(blocks_here, BLK, HEADS, HD)
    list_counts = block_count[0]
    list_blocks = block_list[0]
    slot_count = list_blocks.shape[1]
    offsets = jnp.arange(BLK, dtype=jnp.int32)
    inv_root = 1.0 / HD**0.5
    row_index = (list_blocks[:, :, None] * BLK + offsets[None, None, :]).reshape(-1)
    key_mask = jnp.repeat(
        jnp.arange(slot_count, dtype=jnp.int32)[None, :] < list_counts[:, None], BLK, axis=1
    )
    selected = jnp.take(feature_table, row_index, axis=0)
    key_values = jnp.dot(
        selected,
        lax.all_gather(kv_weight[0], "frames", axis=1, tiled=True),
        preferred_element_type=jnp.float32,
    ).astype(jnp.bfloat16)
    key_heads = key_values[:, :feature_width].reshape(-1, HEADS, HD)
    value_heads = key_values[:, feature_width:].reshape(-1, HEADS, HD)
    keys_part = key_heads.reshape(blocks_here, -1, HEADS, HD)
    values_part = value_heads.reshape(blocks_here, -1, HEADS, HD)
    scores = jnp.einsum("bqhd,bkhd->bhqk", queries, keys_part, preferred_element_type=jnp.float32)
    softmax_scores = scores
    softmax_scores = jnp.where(
        key_mask[:, None, None, :], softmax_scores * inv_root, jnp.float32(-1e30)
    )
    top_score = jnp.max(softmax_scores, axis=-1, keepdims=True)
    expo = jnp.exp(softmax_scores - top_score)
    weights = (expo / jnp.sum(expo, axis=-1, keepdims=True)).astype(jnp.bfloat16)
    mixed_heads = jnp.einsum(
        "bhqk,bkhd->bqhd", weights, values_part, preferred_element_type=jnp.float32
    )
    part_blocks = blocks_here - 0
    mixed_rows = mixed_heads.reshape(part_blocks * BLK, feature_width)
    gate_rows = jnp.repeat(modulate[0:blocks_here, 2], BLK, axis=0)
    result = (stream + gate_rows * mixed_rows).astype(jnp.bfloat16)
    handed = from_behind(result[None], "segment", 1)
    return handed


def solution(mesh):
    placed = (
        P("segment", "frames", None),
        P("frames", None),
        P("segment", None, "frames"),
        P("segment", None, None, None),
        P("segment", "frames"),
        P("segment", "frames", None),
        P("segment", "frames"),
    )
    return jax.shard_map(
        local, mesh=mesh, in_specs=placed, out_specs=P("segment", "frames", None), check_vma=False
    )
```

profile of v0, /device:TPU:32, one launch (start us, length us, event | category | flops | bytes accessed | tf_op | source)
XLA Modules:
  0.0 365.3 jit_solution(4835332354557125818)
XLA Ops:
  6.5 0.0 copy-start
  6.5 0.0 copy-start.3
  6.5 0.0 copy-start.4
  6.5 0.0 all-gather.4.cloned.1.call-start
  6.5 0.7 all-gather.4.cloned.1.call-update
  7.3 0.0 all-gather.6.cloned.1.call-start
  7.3 0.7 all-gather.6.cloned.1.call-update
  8.0 0.7 multiply_bitcast_fusion
  8.7 0.1 iota_add_fusion
  8.8 0.1 add.89
  8.9 0.1 add.86
  8.9 1.6 reshape.134
  10.5 0.7 fusion.21
  11.2 0.0 copy-done.3
  11.2 0.4 multiply_reduce_fusion
  11.6 0.2 fusion.20
  11.8 0.0 copy-done
  11.8 0.2 multiply_reduce_fusion.1
  12.1 0.1 rsqrt.12
  12.1 0.0 copy-done.4
  12.1 0.1 iota_compare_fusion
  12.2 0.1 broadcast_in_dim.41
  12.3 0.1 broadcast_in_dim.42
  12.4 1.4 add_convert_fusion
  13.8 152.8 %all-gather.4.cloned.1.call-done = bf16[4096,768]{1,0:T(8,128)(2,1)} async-done(((bf16[64,768]{1,0:T(8,128)(2,1)}), bf16[4096,768]{1,0:T(8,128)(2,1)}) %all-gather.4.cloned.1.call-update) | async-done | bytes 6291472 | tf_op jit(solution)/shard_map/all_gather | solution.py:18
  166.6 8.1 %gather_fusion = bf16[1024,768]{1,0:T(8,128)(2,1)S(1)} fusion(bf16[4096,768]{1,0:T(8,128)(2,1)} %all-gather.4.cloned.1.call-done, s32[1024]{0:T(1024)S(1)} %broadcast_clamp_fusion), kind=kCustom, calls=%fused_computation | custom fusion | bytes 3149824 | tf_op jit(solution)/shard_map/jit(_take)/gather | solution.py:43
  174.7 137.1 %all-gather.6.cloned.1.call-done = bf16[1,768,3072]{1,2,0:T(8,128)(2,1)} async-done(((bf16[1,768,48]{1,2,0:T(8,128)(2,1)}), bf16[1,768,3072]{1,2,0:T(8,128)(2,1)}) %all-gather.6.cloned.1.call-update) | async-done | bytes 4718608 | tf_op jit(solution)/shard_map/all_gather | solution.py:46
  311.8 7.9 %convolution_convert_fusion = bf16[1024,3072]{1,0:T(8,128)(2,1)S(1)} fusion(bf16[1,768,3072]{1,2,0:T(8,128)(2,1)} %all-gather.6.cloned.1.call-done, bf16[1024,768]{1,0:T(8,128)(2,1)S(1)} %gather_fusion, pred[1024]{0:T(1024)(128)(4,1)S(1)} %compare_and_fusion), kind=kOutput, calls=%fused_computation.2 | convolution fusion | flops 4835770368 | bytes 12583936 | tf_op jit(solution)/shard_map/dot_general | solution.py:44
  319.6 2.2 fusion.25
  321.8 6.9 %reshape.144 = bf16[4,256,12,128]{3,2,1,0:T(8,128)(2,1)} reshape(bf16[1024,1536]{1,0:T(8,128)(2,1)} %get-tuple-element.8) | data formatting | bytes 6291456 | tf_op jit(solution)/shard_map/reshape;reshape | solution.py:52
  328.7 3.6 reshape.145
  332.3 3.7 %fusion.2 = f32[4,12,64,256]{3,2,1,0:T(8,128)S(1)} fusion(bf16[4,256,12,128]{3,2,1,0:T(8,128)(2,1)} %reshape.145, bf16[4,64,12,128]{3,2,1,0:T(8,128)(2,1)} %add_convert_fusion), kind=kOutput, calls=%fused_computation.4 | convolution fusion | flops 201326592 | bytes 7077888 | tf_op jit(solution)/shard_map/bqhd,bkhd->bhqk/dot_general | solution.py:53
  336.0 0.0 copy-start.2
  336.1 1.4 fusion.26
  337.5 0.8 copy-done.2
  338.2 2.4 fusion.15
  340.7 0.9 copy.24
  341.6 0.0 copy-start.1
  341.6 1.4 reshape.133
  343.0 0.2 broadcast_in_dim.38
  343.2 0.0 copy-done.1
  343.2 1.8 fusion.8
  345.0 0.0 collective-permute-start
  345.0 12.6 %collective-permute-done = bf16[1,256,1536]{2,1,0:T(8,128)(2,1)S(1)} collective-permute-done((bf16[1,256,1536]{2,1,0:T(8,128)(2,1)S(1)}, bf16[1,256,1536]{2,1,0:T(8,128)(2,1)S(1)}, u32[]{:S(2)}, u32[]{:S(2)}) %collective-permute-start) | collective-permute-done | bytes 786464 | tf_op jit(solution)/shard_map/ppermute | solution.py:14
  357.6 0.9 copy.41
  (7 shorter events, 0.1 us)
Async XLA Ops:
  6.5 5.3 %copy-start = (bf16[1,256,1536]{2,1,0:T(8,128)(2,1)S(1)}, bf16[1,256,1536]{2,1,0:T(8,128)(2,1)}, u32[]{:S(2)}) copy-start(bf16[1,256,1536]{2,1,0:T(8,128)(2,1)} %param.7) | copy-start | bytes 2359300
  6.5 4.7 %copy-start.3 = (f32[1,32,3,1536]{3,1,2,0:T(8,128)S(1)}, f32[1,32,3,1536]{3,1,2,0:T(8,128)}, u32[]{:S(2)}) copy-start(f32[1,32,3,1536]{3,1,2,0:T(8,128)} %param.10) | copy-start | bytes 1769476
  6.5 5.6 %copy-start.4 = (s32[1,4]{1,0:T(1,128)S(1)}, s32[1,4]{1,0:T(1,128)}, u32[]{:S(2)}) copy-start(s32[1,4]{1,0:T(1,128)} %param.13) | copy-start | bytes 52
  6.5 160.1 %all-gather.4.cloned.1.call-start = ((), (), s32[]{:S(2)}) async-start(), calls=%async_computation | async-start | bytes 6389760 | tf_op jit(solution)/shard_map/all_gather | solution.py:18
  7.3 304.5 %all-gather.6.cloned.1.call-start = ((), (), s32[]{:S(2)}) async-start(), calls=%async_computation.1 | async-start | bytes 4792320 | tf_op jit(solution)/shard_map/all_gather | solution.py:46
  336.0 2.2 copy-start.2
  341.6 1.6 copy-start.1
  345.0 12.6 %collective-permute-start = (bf16[1,256,1536]{2,1,0:T(8,128)(2,1)S(1)}, bf16[1,256,1536]{2,1,0:T(8,128)(2,1)S(1)}, u32[]{:S(2)}, u32[]{:S(2)}) collective-permute-start(bf16[1,256,1536]{2,1,0:T(8,128)(2,1)S(1)} %fusion.8), channel_id=1, source_target_pairs={{448,0},{0,64},{64,128},{128,192},{192,256},{256,320},{320,384},{3... | collective-permute-start | bytes 2359304 | tf_op jit(solution)/shard_map/ppermute | solution.py:14
Sparse Core Ops, SparseCore 0:
  10.3 156.2 all-gather.3
  169.6 142.1 all-gather.5
where the time goes:
time: 366 us; the launch traced here: 365 us
  waiting for transfers between devices  304 us (83%)
  local copies, waits for them, and re-layouts  26.9 us (7%)
  matrix products  14 us (4%)
  between operations  13.6 us (4%)
  other arithmetic  6.91 us (2%)
    all_gather x1, waiting for transfers between devices, local(): feature_table = lax.all_gather(features, 'frames', axis=0, tiled=True)  153 us
    all_gather x1, waiting for transfers between devices, local(): lax.all_gather(kv_weight[0], 'frames', axis=1, tiled=True)  137 us
    ppermute x1, waiting for transfers between devices, from_behind(): return lax.ppermute(block, axis, route)  12.6 us
    gather x1, local copies, waits for them, and re-layouts, local(): selected = jnp.take(feature_table, row_index, axis=0)  8.07 us
    dot_general x1, matrix products, local(): jnp.dot(selected, lax.all_gather(kv_weight[0], 'frames', axis=1, tiled=Tr...  7.88 us
  transfers between devices with their start and end apart: 3, of which 3 were waited for; matrix products, arithmetic and copies ran while one was open for 4% of the time, Pallas kernels for 0%

commit v1 on v0

--- a/solution.py
+++ b/solution.py
@@ -43,7 +43,10 @@
     selected = jnp.take(feature_table, row_index, axis=0)
     key_values = jnp.dot(
         selected,
-        lax.all_gather(kv_weight[0], "frames", axis=1, tiled=True),
+        jnp.concatenate(
+            lax.all_to_all(jnp.stack([kv_weight[0]] * lax.axis_size("frames")), "frames", 0, 0),
+            axis=1,
+        ),
         preferred_element_type=jnp.float32,
     ).astype(jnp.bfloat16)
     key_heads = key_values[:, :feature_width].reshape(-1, HEADS, HD)

time: 366 us -> 346 us (0.945)
  the two profiles are of different devices: /device:TPU:32 before, /device:TPU:24 now
where the time goes in v1:
time: 346 us
  waiting for transfers between devices  264 us (76%)
  local copies, waits for them, and re-layouts  29.2 us (8%)
  starting transfers between devices  19.1 us (6%)
  matrix products  14 us (4%)
  between operations  13.6 us (4%)
  other arithmetic  5.59 us (2%)
    all_gather x1, waiting for transfers between devices, local(): feature_table = lax.all_gather(features, 'frames', axis=0, tiled=True)  251 us
    all_to_all x1, starting transfers between devices, local(): lax.all_to_all(jnp.stack([kv_weight[0]] * lax.axis_size('frames')), 'fram...  19 us
    ppermute x1, waiting for transfers between devices, from_behind(): return lax.ppermute(block, axis, route)  12.6 us
    gather x1, local copies, waits for them, and re-layouts, local(): selected = jnp.take(feature_table, row_index, axis=0)  8.07 us
    dot_general x1, matrix products, local(): jnp.dot(selected, jnp.concatenate(lax.all_to_all(jnp.stack([kv_weight[0]]...  7.9 us
  transfers between devices with their start and end apart: 3, of which 2 were waited for; matrix products, arithmetic and copies ran while one was open for 3% of the time, Pallas kernels for 0%

profile of v1, /device:TPU:24, one launch (start us, length us, event | category | flops | bytes accessed | tf_op | source)
XLA Modules:
  0.0 345.8 jit_solution(13985157988148393152)
XLA Ops:
  6.5 3.4 stack.3
  9.9 0.0 copy-start.4
  9.9 0.0 copy-start
  9.9 0.0 copy-start.5
  9.9 19.0 %all-to-all-start = ((bf16[64,768,48]{1,2,0:T(8,128)(2,1)}), bf16[64,768,48]{1,2,0:T(8,128)(2,1)}, u32[]{:S(2)}, u32[]{:S(2)}) async-start(bf16[64,768,48]{1,2,0:T(8,128)(2,1)} %stack.3), calls=%async_computation | async-start | bytes 9437184 | tf_op jit(solution)/shard_map/all_to_all | solution.py:47
  28.9 0.0 copy-start.3
  29.0 0.0 copy-start.6
  29.0 0.0 all-gather.2.cloned.1.call-start
  29.0 0.7 all-gather.2.cloned.1.call-update
  29.7 0.0 copy-done.4
  29.7 0.1 iota_add_fusion
  29.8 0.1 add.89
  29.9 0.1 add.86
  30.0 0.0 copy-done
  30.0 0.5 reshape.143
  30.4 0.0 copy-done.5
  30.5 0.1 fusion.20
  30.5 0.0 copy-done.3
  30.5 0.4 multiply_reduce_fusion
  30.9 0.2 fusion.19
  31.1 0.2 multiply_reduce_fusion.1
  31.3 0.1 rsqrt.12
  31.4 0.0 copy-done.6
  31.4 0.1 iota_compare_fusion
  31.5 0.1 broadcast_in_dim.41
  31.6 0.1 broadcast_in_dim.42
  31.7 1.4 add_convert_fusion
  33.1 251.0 %all-gather.2.cloned.1.call-done = bf16[4096,768]{1,0:T(8,128)(2,1)} async-done(((bf16[64,768]{1,0:T(8,128)(2,1)}), bf16[4096,768]{1,0:T(8,128)(2,1)}) %all-gather.2.cloned.1.call-update) | async-done | bytes 6291472 | tf_op jit(solution)/shard_map/all_gather | solution.py:18
  284.1 8.1 %gather_fusion = bf16[1024,768]{1,0:T(8,128)(2,1)S(1)} fusion(bf16[4096,768]{1,0:T(8,128)(2,1)} %all-gather.2.cloned.1.call-done, s32[1024]{0:T(1024)S(1)} %broadcast_clamp_fusion), kind=kCustom, calls=%fused_computation | custom fusion | bytes 3149824 | tf_op jit(solution)/shard_map/jit(_take)/gather | solution.py:43
  292.2 0.0 all-to-all-done
  292.2 7.9 %convolution_convert_fusion = bf16[1024,3072]{1,0:T(8,128)(2,1)S(1)} fusion(bf16[768,3072]{0,1:T(8,128)(2,1)} %bitcast.7, bf16[1024,768]{1,0:T(8,128)(2,1)S(1)} %gather_fusion, pred[1024]{0:T(1024)(128)(4,1)S(1)} %compare_and_fusion), kind=kOutput, calls=%fused_computation.2 | convolution fusion | flops 4835770368 | bytes 12583936 | tf_op jit(solution)/shard_map/dot_general | solution.py:44
  300.1 2.2 fusion.24
  302.3 6.9 %reshape.152 = bf16[4,256,12,128]{3,2,1,0:T(8,128)(2,1)} reshape(bf16[1024,1536]{1,0:T(8,128)(2,1)} %get-tuple-element.8) | data formatting | bytes 6291456 | tf_op jit(solution)/shard_map/reshape;reshape | solution.py:55
  309.1 3.6 %reshape.153 = bf16[4,256,12,128]{3,2,1,0:T(8,128)(2,1)} reshape(bf16[1024,1536]{1,0:T(8,128)(2,1)S(1)} %get-tuple-element.7) | data formatting | bytes 6291456 | tf_op jit(solution)/shard_map/reshape;reshape | solution.py:54
  312.8 3.7 %fusion.1 = f32[4,12,64,256]{3,2,1,0:T(8,128)S(1)} fusion(bf16[4,256,12,128]{3,2,1,0:T(8,128)(2,1)} %reshape.153, bf16[4,64,12,128]{3,2,1,0:T(8,128)(2,1)} %add_convert_fusion), kind=kOutput, calls=%fused_computation.3 | convolution fusion | flops 201326592 | bytes 7077888 | tf_op jit(solution)/shard_map/bqhd,bkhd->bhqk/dot_general | solution.py:56
  316.5 0.0 copy-start.2
  316.5 1.4 fusion.25
  317.9 0.8 copy-done.2
  318.7 2.4 fusion.14
  321.1 0.9 copy.25
  322.0 0.0 copy-start.1
  322.1 1.4 reshape.142
  323.4 0.2 broadcast_in_dim.38
  323.6 0.0 copy-done.1
  323.6 1.8 fusion.7
  325.4 0.0 collective-permute-start
  325.4 12.6 %collective-permute-done = bf16[1,256,1536]{2,1,0:T(8,128)(2,1)S(1)} collective-permute-done((bf16[1,256,1536]{2,1,0:T(8,128)(2,1)S(1)}, bf16[1,256,1536]{2,1,0:T(8,128)(2,1)S(1)}, u32[]{:S(2)}, u32[]{:S(2)}) %collective-permute-start) | collective-permute-done | bytes 786464 | tf_op jit(solution)/shard_map/ppermute | solution.py:14
  338.1 0.9 copy.42
  (8 shorter events, 0.1 us)
Async XLA Ops:
  9.9 19.8 %copy-start.4 = (s32[1,4,4]{2,1,0:T(4,128)S(1)}, s32[1,4,4]{2,1,0:T(4,128)}, u32[]{:S(2)}) copy-start(s32[1,4,4]{2,1,0:T(4,128)} %param.12) | copy-start | bytes 196
  9.9 20.0 %copy-start = (bf16[1,256,1536]{2,1,0:T(8,128)(2,1)S(1)}, bf16[1,256,1536]{2,1,0:T(8,128)(2,1)}, u32[]{:S(2)}) copy-start(bf16[1,256,1536]{2,1,0:T(8,128)(2,1)} %param.7) | copy-start | bytes 2359300
  9.9 20.5 %copy-start.5 = (s32[1,4]{1,0:T(1,128)S(1)}, s32[1,4]{1,0:T(1,128)}, u32[]{:S(2)}) copy-start(s32[1,4]{1,0:T(1,128)} %param.11) | copy-start | bytes 52
  9.9 282.2 %all-to-all-start = ((bf16[64,768,48]{1,2,0:T(8,128)(2,1)}), bf16[64,768,48]{1,2,0:T(8,128)(2,1)}, u32[]{:S(2)}, u32[]{:S(2)}) async-start(bf16[64,768,48]{1,2,0:T(8,128)(2,1)} %stack.3), calls=%async_computation | async-start | bytes 9437184 | tf_op jit(solution)/shard_map/all_to_all | solution.py:47
  28.9 1.6 copy-start.3
  29.0 2.5 copy-start.6
  29.0 255.1 %all-gather.2.cloned.1.call-start = ((), (), s32[]{:S(2)}) async-start(), calls=%async_computation.1 | async-start | bytes 6389760 | tf_op jit(solution)/shard_map/all_gather | solution.py:18
  316.5 2.2 copy-start.2
  322.0 1.6 copy-start.1
  325.4 12.6 %collective-permute-start = (bf16[1,256,1536]{2,1,0:T(8,128)(2,1)S(1)}, bf16[1,256,1536]{2,1,0:T(8,128)(2,1)S(1)}, u32[]{:S(2)}, u32[]{:S(2)}) collective-permute-start(bf16[1,256,1536]{2,1,0:T(8,128)(2,1)S(1)} %fusion.7), channel_id=1, source_target_pairs={{448,0},{0,64},{64,128},{128,192},{192,256},{256,320},{320,384},{3... | collective-permute-start | bytes 2359304 | tf_op jit(solution)/shard_map/ppermute | solution.py:14
Sparse Core Ops, SparseCore 0:
  32.8 251.2 all-gather.1
